TPU v7x, 32 devices: a whole 2x2x4 slice. The times are simulated.
32 devices in a mesh: col: 8 (over y, x, core), row: 4 (over z).
Axes of the slice: x: 2, y: 2, z: 4, core: 2. Of those that a mesh axis runs over, the one named last changes fastest.
Arguments:
- samples_x: bfloat16 [512, 98304], P('row', 'col'), may hold values from -6 to 6
- targets: bfloat16 [512, 98304], P('row', 'col'), may hold values from -6 to 6
- times: int32 [512], P('row'), may hold values from 0 to 63
- block_rows: int32 [576], P(('col', 'row')), may hold values from 0 to 767, as said below
- block_cols: int32 [576], P(('col', 'row')), may hold values from 0 to 767, as said below
Outputs:
- coeffs: float32 [576, 128, 128], P(('col', 'row'))
- residual: float32 [512, 98304], P('row', 'col')
Inputs may be any that keep to these rules, and one draw needn't show every extreme that they name: `block_rows`: the blocks are listed by column group (the 96 column blocks c * 96 to (c + 1) * 96 - 1 form group c), and within a group in 8 runs of 9 blocks, run g holding row blocks of group g; no block appears twice. `block_cols`: each block's column block lies in the group of its place in the list, as described for block_rows.
All inputs are finite; a program needn't handle non-finite values.
Results may differ from a plain program's by a relative error of at most 0.009.
Values may be sent and summed in bfloat16 or wider, within the bound.
A program may use at most 192 MiB of HBM per device.

v0:
```python
import functools
import math

import jax
import jax.numpy as jnp
from jax import lax
from jax.experimental import pallas as pl
from jax.experimental.pallas import tpu as pltpu
from jax.sharding import PartitionSpec as P

BLOCK = 128
T_STEPS = 64
RIDGE_SHARE = 0.2
LANES = 128
LAG = 2
VMEM = pltpu.VMEM
F32 = jnp.float32
BF16 = jnp.bfloat16
WHOLE = pl.BlockSpec(memory_space=pltpu.VMEM)
SCALARS = pl.BlockSpec(memory_space=pltpu.SMEM)


def enter(axes):
    barrier = pltpu.get_barrier_semaphore()
    count = 0
    for axis in axes:
        n = lax.axis_size(axis)
        me = lax.axis_index(axis)
        for k in range(1, n):
            pl.semaphore_signal(
                barrier, inc=1, device_id={axis: lax.rem(me + k, n)},
                device_id_type=pl.DeviceIdType.MESH,
            )
        count += n - 1
    pl.semaphore_wait(barrier, count)


def push(src, dst, send, recv, axis, k):
    n = lax.axis_size(axis)
    return pltpu.make_async_remote_copy(
        src_ref=src, dst_ref=dst, send_sem=send, recv_sem=recv,
        device_id={axis: lax.rem(lax.axis_index(axis) + k, n)},
        device_id_type=pl.DeviceIdType.MESH,
    )


def gather_small_kernel(x_ref, out_ref, send_c, recv_c, send_r, recv_r):
    cols, rows = lax.axis_size("col"), lax.axis_size("row")
    my_col, my_row = lax.axis_index("col"), lax.axis_index("row")
    enter(("col", "row"))
    out_ref[my_row, my_col] = x_ref[...]
    first = [
        push(x_ref, out_ref.at[my_row, my_col], send_c.at[k - 1], recv_c.at[k - 1], "col", k)
        for k in range(1, cols)
    ]
    for copy in first:
        copy.start()
    for copy in first:
        copy.wait()
    second = [
        push(out_ref.at[my_row], out_ref.at[my_row], send_r.at[k - 1], recv_r.at[k - 1], "row", k)
        for k in range(1, rows)
    ]
    for copy in second:
        copy.start()
    for copy in second:
        copy.wait()


def gather_small(x, call_id):
    cols, rows = lax.axis_size("col"), lax.axis_size("row")
    return pl.pallas_call(
        gather_small_kernel,
        out_shape=jax.ShapeDtypeStruct((rows, cols) + x.shape, x.dtype),
        in_specs=[WHOLE],
        out_specs=WHOLE,
        scratch_shapes=[
            pltpu.SemaphoreType.DMA((cols - 1,)), pltpu.SemaphoreType.DMA((cols - 1,)),
            pltpu.SemaphoreType.DMA((rows - 1,)), pltpu.SemaphoreType.DMA((rows - 1,)),
        ],
        compiler_params=pltpu.CompilerParams(collective_id=call_id, has_side_effects=True),
    )(x)


def select_kernel(run, index_ref, x_ref, out_ref):
    def one(b, carry):
        column = pl.multiple_of(index_ref[b] * BLOCK, BLOCK)
        out_ref[b] = x_ref[:, pl.ds(column, BLOCK)]
        return carry

    lax.fori_loop(0, out_ref.shape[0], one, 0, unroll=2)


def select_blocks(index, x):
    count = index.shape[0]
    return pl.pallas_call(
        functools.partial(select_kernel, count),
        out_shape=jax.ShapeDtypeStruct((count, x.shape[0], BLOCK), x.dtype),
        in_specs=[SCALARS, WHOLE],
        out_specs=WHOLE,
    )(index, x)


def exchange_kernel(run, x_ref, out_ref, send, recv):
    n, me = lax.axis_size("col"), lax.axis_index("col")
    enter(("col",))
    copies = []
    for k in range(1, n):
        peer = lax.rem(me + k, n)
        copies.append(
            push(x_ref.at[pl.ds(peer * run, run)], out_ref.at[pl.ds(me * run, run)],
                 send.at[k - 1], recv.at[k - 1], "col", k)
        )
    for copy in copies:
        copy.start()

    def own(i, carry):
        out_ref[me * run + i] = x_ref[me * run + i]
        return carry

    lax.fori_loop(0, run, own, 0)
    for copy in copies:
        copy.wait()


def exchange_blocks(x, call_id):
    n = lax.axis_size("col")
    return pl.pallas_call(
        functools.partial(exchange_kernel, x.shape[0] // n),
        out_shape=jax.ShapeDtypeStruct(x.shape, x.dtype),
        in_specs=[WHOLE],
        out_specs=WHOLE,
        scratch_shapes=[pltpu.SemaphoreType.DMA((n - 1,)), pltpu.SemaphoreType.DMA((n - 1,))],
        compiler_params=pltpu.CompilerParams(collective_id=call_id, has_side_effects=True),
    )(x)


def block_dot(x, e):
    return lax.dot_general(x, e, (((0,), (0,)), ((), ())), preferred_element_type=F32)


def unroll_of(count):
    return math.gcd(count, 8)


def first_terms_kernel(cols_ref, x_ref, t_ref, w_ref, out_ref):
    count = x_ref.shape[0]
    step = unroll_of(count)

    def some(i, carry):
        for j in range(step):
            b = i * step + j
            place = pl.ds(pl.multiple_of(cols_ref[b] * BLOCK, BLOCK), BLOCK)
            e = (t_ref[:, place].astype(F32) * w_ref[...]).astype(BF16)
            out_ref[b] = block_dot(x_ref[b], e).astype(BF16)
        return carry

    lax.fori_loop(0, count // step, some, 0)


def first_terms(cols, x, targets, weight):
    return pl.pallas_call(
        first_terms_kernel,
        out_shape=jax.ShapeDtypeStruct((x.shape[0], BLOCK, BLOCK), BF16),
        in_specs=[SCALARS, WHOLE, WHOLE, WHOLE],
        out_specs=WHOLE,
    )(cols, x, targets, weight)


def next_terms_kernel(cols_ref, scale_ref, x_ref, t_ref, image_ref, w_ref, out_ref):
    count = x_ref.shape[0]
    step = unroll_of(count)
    alpha = scale_ref[0]

    def some(i, carry):
        for j in range(step):
            b = i * step + j
            place = pl.ds(pl.multiple_of(cols_ref[b] * BLOCK, BLOCK), BLOCK)
            left = t_ref[:, place].astype(F32) - alpha * image_ref[:, place]
            out_ref[b] = block_dot(x_ref[b], (left * w_ref[...]).astype(BF16)).astype(BF16)
        return carry

    lax.fori_loop(0, count // step, some, 0)


def next_terms(cols, scale, x, targets, image, weight):
    return pl.pallas_call(
        next_terms_kernel,
        out_shape=jax.ShapeDtypeStruct((x.shape[0], BLOCK, BLOCK), BF16),
        in_specs=[SCALARS, SCALARS, WHOLE, WHOLE, WHOLE, WHOLE],
        out_specs=WHOLE,
    )(cols, scale, x, targets, image, weight)


def sweep_kernel(first, *refs):
    if first:
        (terms_ref, out_ref, own_ref, sums_ref, from_left, from_right, to_right, to_left,
         send_r, recv_r, send_l, recv_l) = refs
        before_ref = None
    else:
        (scale_ref, terms_ref, before_ref, out_ref, own_ref, sums_ref, from_left, from_right,
         to_right, to_left, send_r, recv_r, send_l, recv_l) = refs
        shift = scale_ref[1]
    n, me = lax.axis_size("row"), lax.axis_index("row")
    pieces = send_r.shape[0]
    size = terms_ref.shape[0] // pieces
    share = own_ref.shape[0]
    has_left, has_right = me > 0, me < n - 1
    barrier = pltpu.get_barrier_semaphore()

    def greet(k):
        pl.semaphore_signal(
            barrier, inc=1, device_id={"row": lax.rem(me + k, n)},
            device_id_type=pl.DeviceIdType.MESH,
        )

    pl.when(has_left)(lambda: greet(n - 1))
    pl.when(has_right)(lambda: greet(1))
    pl.semaphore_wait(barrier, has_left.astype(jnp.int32) + has_right.astype(jnp.int32))

    def rightward(src, p):
        place = pl.ds(p * size, size)
        return push(src.at[place], from_left.at[place], send_r.at[p], recv_r.at[p], "row", 1)

    def leftward(src, p):
        place = pl.ds(p * size, size)
        return push(src.at[place], from_right.at[place], send_l.at[p], recv_l.at[p], "row", n - 1)

    def begin(source, heading):
        def one(p, carry):
            heading(source, p).start()
            return carry

        lax.fori_loop(0, pieces, one, 0)

    def clear(buffer):
        def one(i, carry):
            buffer[i] = jnp.zeros((BLOCK, BLOCK), BF16)
            return carry

        lax.fori_loop(0, buffer.shape[0], one, 0)

    @pl.when(me == 0)
    def _():
        begin(terms_ref, rightward)
        clear(from_left)

    @pl.when(me == n - 1)
    def _():
        begin(terms_ref, leftward)
        clear(from_right)

    def add(arrived, staged, p):
        def one(i, carry):
            b = p * size + i
            staged[b] = (arrived[b].astype(F32) + terms_ref[b].astype(F32)).astype(BF16)
            return carry

        lax.fori_loop(0, size, one, 0)

    def total_of(b):
        total = terms_ref[b].astype(F32) + from_left[b].astype(F32) + from_right[b].astype(F32)
        if before_ref is not None:
            total = total - shift * before_ref[b].astype(F32)
        return total

    def pass_right(p):
        @pl.when(has_left)
        def _():
            rightward(to_right, p).wait_recv()

            @pl.when(has_right)
            def _():
                add(from_left, to_right, p)
                rightward(to_right, p).start()

    def pass_left(p):
        @pl.when(has_right)
        def _():
            leftward(to_left, p).wait_recv()

            @pl.when(has_left)
            def _():
                add(from_right, to_left, p)
                leftward(to_left, p).start()

    low = me * 2 < n

    def piece(q, carry):
        @pl.when(q < pieces)
        def _():
            pl.when(low)(lambda: pass_right(q))
            pl.when(jnp.logical_not(low))(lambda: pass_left(q))

        @pl.when(q >= LAG)
        def _():
            p = q - LAG
            pl.when(low)(lambda: pass_left(p))
            pl.when(jnp.logical_not(low))(lambda: pass_right(p))

            def one(i, inner):
                b = p * size + i
                out_ref[b] = total_of(b).astype(BF16)
                return inner

            lax.fori_loop(0, size, one, 0)

        return carry

    lax.fori_loop(0, pieces + LAG, piece, 0)
    sums_ref[...] = jnp.zeros_like(sums_ref)

    def own(i, carry):
        b = me * share + i
        total = total_of(b)
        rounded = total.astype(BF16)
        own_ref[i] = rounded
        wide = rounded.astype(F32)
        sums_ref[0:1, :] += jnp.sum(total * total, axis=0, keepdims=True)
        sums_ref[1:2, :] += jnp.sum(wide * wide, axis=0, keepdims=True)
        if before_ref is not None:
            flat = before_ref[b].astype(F32)
            sums_ref[2:3, :] += jnp.sum(wide * flat, axis=0, keepdims=True)
        return carry

    lax.fori_loop(0, share, own, 0)

    def finish(p, carry):
        pl.when(has_right)(lambda: rightward(to_right, p).wait_send())
        pl.when(has_left)(lambda: leftward(to_left, p).wait_send())
        return carry

    lax.fori_loop(0, pieces, finish, 0)


def sweep(terms, scale, before, call_id):
    n = lax.axis_size("row")
    share = terms.shape[0] // n
    pieces = math.gcd(terms.shape[0], 24)
    first = before is None
    sems = pltpu.SemaphoreType.DMA((pieces,))
    whole = VMEM(terms.shape, BF16)
    return pl.pallas_call(
        functools.partial(sweep_kernel, first),
        out_shape=(
            jax.ShapeDtypeStruct(terms.shape, BF16),
            jax.ShapeDtypeStruct((share, BLOCK, BLOCK), BF16),
            jax.ShapeDtypeStruct((8, LANES), F32),
        ),
        in_specs=[WHOLE] if first else [SCALARS, WHOLE, WHOLE],
        out_specs=(WHOLE, WHOLE, WHOLE),
        scratch_shapes=[whole, whole, whole, whole, sems, sems, sems, sems],
        compiler_params=pltpu.CompilerParams(collective_id=call_id, has_side_effects=True),
    )(*((terms,) if first else (scale, terms, before)))


def apply_kernel(first, cols_ref, x_ref, d_ref, w_ref, *refs):
    if first:
        image_ref, sums_ref = refs
        before_ref = None
    else:
        before_ref, image_ref, sums_ref = refs
    count = x_ref.shape[0]
    step = unroll_of(count)
    columns = image_ref.shape[1] // BLOCK
    samples = image_ref.shape[0]

    def clear(i, carry):
        place = pl.ds(pl.multiple_of(i * BLOCK, BLOCK), BLOCK)
        image_ref[:, place] = jnp.zeros((samples, BLOCK), F32)
        return carry

    lax.fori_loop(0, columns, clear, 0, unroll=4)

    def some(i, carry):
        made = [
            jnp.dot(x_ref[i * step + j], d_ref[i * step + j], preferred_element_type=F32)
            for j in range(step)
        ]
        for j in range(step):
            place = pl.ds(pl.multiple_of(cols_ref[i * step + j] * BLOCK, BLOCK), BLOCK)
            image_ref[:, place] += made[j]
        return carry

    lax.fori_loop(0, count // step, some, 0)

    def fold(values):
        return jnp.sum(values.reshape(samples // 8, 8, BLOCK), axis=0)

    def measure(i, carry):
        place = pl.ds(pl.multiple_of(i * BLOCK, BLOCK), BLOCK)
        image = image_ref[:, place]
        weighted = w_ref[...] * image
        square, cross = carry
        square = square + fold(weighted * image)
        if before_ref is not None:
            cross = cross + fold(weighted * before_ref[:, place])
        return square, cross

    empty = jnp.zeros((8, BLOCK), F32)
    square, cross = lax.fori_loop(0, columns, measure, (empty, empty), unroll=4)
    sums_ref[...] = jnp.zeros_like(sums_ref)
    sums_ref[0:1, :] = jnp.sum(square, axis=0, keepdims=True)
    sums_ref[1:2, :] = jnp.sum(cross, axis=0, keepdims=True)


def apply_blocks(cols, x, direction, weight, before, taxa):
    first = before is None
    samples = x.shape[1]
    return pl.pallas_call(
        functools.partial(apply_kernel, first),
        out_shape=(
            jax.ShapeDtypeStruct((samples, taxa), F32),
            jax.ShapeDtypeStruct((8, LANES), F32),
        ),
        in_specs=[SCALARS] + [WHOLE] * (3 if first else 4),
        out_specs=(WHOLE, WHOLE),
    )(cols, x, direction, weight, *(() if first else (before,)))


def on_device(samples_x, targets, times, block_rows, block_cols):
    col_count = lax.axis_size("col")
    row_count = lax.axis_size("row")
    taxa_col = samples_x.shape[1]
    sample_count = samples_x.shape[0]
    column_count = taxa_col // BLOCK
    my_col = lax.axis_index("col")
    shard = block_rows.shape[0]
    group_count = shard * row_count
    run = group_count // col_count
    ridge = RIDGE_SHARE * sample_count * row_count
    weight = jnp.broadcast_to(
        (0.5 + times.astype(F32) / T_STEPS)[:, None], (sample_count, BLOCK)
    )
    places = jnp.pad(
        jnp.stack([block_rows, block_cols]), ((0, 6), (0, LANES - shard))
    )
    everywhere = gather_small(places, 1)
    rows_all = everywhere[:, :, 0, :shard].transpose(1, 0, 2).reshape(col_count, group_count)
    wanted = lax.dynamic_slice_in_dim(rows_all, my_col * run, run, 1) - my_col * column_count
    cols_mine = lax.dynamic_index_in_dim(everywhere[:, :, 1, :shard], my_col, 1, keepdims=False)
    cols = cols_mine.reshape(group_count) - my_col * column_count

    x = exchange_blocks(select_blocks(wanted.reshape(-1), samples_x), 2)
    terms = first_terms(cols, x, targets, weight)
    direction, own0, sums0 = sweep(terms, None, None, 3)
    image0, norms0 = apply_blocks(cols, x, direction, weight, None, taxa_col)
    totals = jnp.sum(
        gather_small(jnp.concatenate([sums0[:2], norms0[:1], jnp.zeros((5, LANES), F32)]), 4),
        axis=(0, 1, 3),
    )
    gamma, flat_norm, image_norm = totals[0], totals[1], totals[2]
    alpha0 = gamma / (image_norm + ridge * flat_norm)
    scale = jnp.stack([alpha0, ridge * alpha0])
    terms = next_terms(cols, scale, x, targets, image0, weight)
    spread, own1, sums1 = sweep(terms, scale, direction, 5)
    image1, norms1 = apply_blocks(cols, x, spread, weight, image0, taxa_col)
    totals = jnp.sum(
        gather_small(jnp.concatenate([sums1[:3], norms1[:2], jnp.zeros((3, LANES), F32)]), 6),
        axis=(0, 1, 3),
    )
    beta = totals[0] / gamma
    flat_next = totals[1] + 2.0 * beta * totals[2] + beta * beta * flat_norm
    image_next = totals[3] + 2.0 * beta * totals[4] + beta * beta * image_norm
    alpha1 = totals[0] / (image_next + ridge * flat_next)
    mixed = alpha0 + alpha1 * beta
    coeffs = mixed * own0.astype(F32) + alpha1 * own1.astype(F32)
    residual = targets.astype(F32) - mixed * image0 - alpha1 * image1
    return (coeffs, residual)


def solution(mesh):
    placed = (P("row", "col"), P("row", "col"), P("row"), P(("col", "row")), P(("col", "row")))
    return jax.shard_map(
        on_device,
        mesh=mesh,
        in_specs=placed,
        out_specs=(P(("col", "row"), None, None), P("row", "col")),
        check_vma=False,
    )
```

profile of v0, /device:TPU:0, one launch (start us, length us, event | category | flops | bytes accessed | tf_op | source)
XLA Modules:
  0.0 272.7 jit_solution(13258393541523457038)
XLA Ops:
  1.5 0.7 pad_add_fusion
  2.7 0.7 broadcast_in_dim.12.w_ref
  3.4 14.4 %shard_map.68 = s32[4,8,8,128]{3,2,1,0:T(8,128)} custom-call(s32[8,128]{1,0:T(8,128)} %pad.4.x_ref), custom_call_target="tpu_custom_call" | custom-call | tf_op jit(solution)/shard_map/pallas_call | solution.py:72
  17.9 1.0 fusion
  20.4 4.1 %shard_map.69.x_ref = bf16[72,128,128]{2,1,0:T(8,128)(2,1)} custom-call(s32[72]{0:T(128)} %reshape.18.index_ref, bf16[128,12288]{1,0:T(8,128)(2,1)} %x_ref.1), custom_call_target="tpu_custom_call" | custom-call | tf_op jit(solution)/shard_map/pallas_call | solution.py:96
  24.5 30.4 %shard_map.70.x_ref = bf16[72,128,128]{2,1,0:T(8,128)(2,1)} custom-call(bf16[72,128,128]{2,1,0:T(8,128)(2,1)} %shard_map.69.x_ref), custom_call_target="tpu_custom_call" | custom-call | tf_op jit(solution)/shard_map/pallas_call | solution.py:128
  55.0 6.4 %shard_map.71.refs_0_ = bf16[72,128,128]{2,1,0:T(8,128)(2,1)} custom-call(s32[72]{0:T(128)} %sub.22.cols_ref, bf16[72,128,128]{2,1,0:T(8,128)(2,1)} %shard_map.70.x_ref, bf16[128,12288]{1,0:T(8,128)(2,1)} %t_ref.3, f32[128,128]{1,0:T(8,128)} %broadcast_in_dim.12.w_ref), custom_call_target="tpu_custom_call" | custom-call | tf_op jit(solution)/shard_map/pallas_call | solution.py:162
  61.4 67.6 %shard_map.72 = (bf16[72,128,128]{2,1,0:T(8,128)(2,1)}, bf16[18,128,128]{2,1,0:T(8,128)(2,1)}, f32[8,128]{1,0:T(8,128)}) custom-call(bf16[72,128,128]{2,1,0:T(8,128)(2,1)} %shard_map.71.refs_0_), custom_call_target="tpu_custom_call" | custom-call | tf_op jit(solution)/shard_map/pallas_call | solution.py:343
  129.0 0.7 slice.45
  129.7 9.1 %shard_map.73 = (f32[128,12288]{1,0:T(8,128)}, f32[8,128]{1,0:T(8,128)}) custom-call(s32[72]{0:T(128)} %sub.22.cols_ref, bf16[72,128,128]{2,1,0:T(8,128)(2,1)} %shard_map.70.x_ref, bf16[72,128,128]{2,1,0:T(8,128)(2,1)} %get-tuple-element.13.d_ref.refs_2_, f32[128,128]{1,0:T(8,128)} %broadcast_in_dim.12.w_ref), custom_call_target="tpu_custom_call" | custom-call | tf_op jit(solution)/shard_map/pallas_call | solution.py:410
  138.7 0.7 slice.46
  140.1 11.4 %shard_map.74 = f32[4,8,8,128]{3,2,1,0:T(8,128)} custom-call(f32[8,128]{1,0:T(8,128)} %maximum_maximum_fusion.x_ref), custom_call_target="tpu_custom_call" | custom-call | tf_op jit(solution)/shard_map/pallas_call | solution.py:72
  151.4 1.1 reduce_sum.18
  155.6 8.5 %shard_map.75.refs_1_ = bf16[72,128,128]{2,1,0:T(8,128)(2,1)} custom-call(s32[72]{0:T(128)} %sub.22.cols_ref, f32[2]{0:T(128)} %pad_maximum_fusion.scale_ref.refs_0_, bf16[72,128,128]{2,1,0:T(8,128)(2,1)} %shard_map.70.x_ref, bf16[128,12288]{1,0:T(8,128)(2,1)} %t_ref.3, f32[128,12288]{1,0:T(8,128)} %get-tuple-element.15.image_ref.refs_0_, ...), custom_call_target="tpu_custom_call" | custom-call | tf_op jit(solution)/shard_map/pallas_call | solution.py:187
  164.1 67.0 %shard_map.76 = (bf16[72,128,128]{2,1,0:T(8,128)(2,1)}, bf16[18,128,128]{2,1,0:T(8,128)(2,1)}, f32[8,128]{1,0:T(8,128)}) custom-call(f32[2]{0:T(128)} %pad_maximum_fusion.scale_ref.refs_0_, bf16[72,128,128]{2,1,0:T(8,128)(2,1)} %shard_map.75.refs_1_, bf16[72,128,128]{2,1,0:T(8,128)(2,1)} %get-tuple-element.13.d_ref.refs_2_), custom_call_target="tpu_custom_call" | custom-call | tf_op jit(solution)/shard_map/pallas_call | solution.py:343
  231.1 0.7 slice.50
  231.8 11.8 %shard_map.77 = (f32[128,12288]{1,0:T(8,128)}, f32[8,128]{1,0:T(8,128)}) custom-call(s32[72]{0:T(128)} %sub.22.cols_ref, bf16[72,128,128]{2,1,0:T(8,128)(2,1)} %shard_map.70.x_ref, bf16[72,128,128]{2,1,0:T(8,128)(2,1)} %get-tuple-element.17.d_ref, f32[128,128]{1,0:T(8,128)} %broadcast_in_dim.12.w_ref, f32[128,12288]{1,0:T(8,128)} %get-tuple-element.15.image_ref.refs_0_), custom_call_target="tpu_custom_call" | custom-call | tf_op jit(solution)/shard_map/pallas_call | solution.py:410
  243.6 0.7 slice.51
  244.3 0.7 maximum_maximum_fusion.1.x_ref
  244.9 10.4 %shard_map.78 = f32[4,8,8,128]{3,2,1,0:T(8,128)} custom-call(f32[8,128]{1,0:T(8,128)} %maximum_maximum_fusion.1.x_ref), custom_call_target="tpu_custom_call" | custom-call | tf_op jit(solution)/shard_map/pallas_call | solution.py:72
  255.4 1.1 reduce_sum.19
  256.4 0.7 fusion.1
  262.9 8.6 %multiply_subtract_fusion = f32[128,12288]{1,0:T(8,128)} fusion(f32[128,12288]{1,0:T(8,128)} %get-tuple-element.21, f32[128,12288]{1,0:T(8,128)} %get-tuple-element.15.image_ref.refs_0_, bf16[128,12288]{1,0:T(8,128)(2,1)S(1)} %copy-done, f32[]{:T(128)S(6)} %div.19, f32[]{:T(128)S(6)} %add.49), kind=kLoop, calls=%fused_computation | loop fusion | flops 7864320 | bytes 22020104 | tf_op jit(solution)/shard_map/sub | solution.py:468
  271.5 1.2 multiply_add_fusion
  (21 shorter events, 4.8 us)
Async XLA Ops:
  231.8 31.0 %copy-start = (bf16[128,12288]{1,0:T(8,128)(2,1)S(1)}, bf16[128,12288]{1,0:T(8,128)(2,1)}, u32[]{:S(2)}) copy-start(bf16[128,12288]{1,0:T(8,128)(2,1)} %t_ref.3) | copy-start | bytes 9437188
  262.8 8.6 %copy-start.1 = (bf16[18,128,128]{2,1,0:T(8,128)(2,1)S(1)}, bf16[18,128,128]{2,1,0:T(8,128)(2,1)}, u32[]{:S(2)}) copy-start(bf16[18,128,128]{2,1,0:T(8,128)(2,1)} %get-tuple-element.19) | copy-start | bytes 1769476
  262.8 8.6 %copy-start.2 = (bf16[18,128,128]{2,1,0:T(8,128)(2,1)S(1)}, bf16[18,128,128]{2,1,0:T(8,128)(2,1)}, u32[]{:S(2)}) copy-start(bf16[18,128,128]{2,1,0:T(8,128)(2,1)} %get-tuple-element.20) | copy-start | bytes 1769476
where the time goes:
time: 273 us
  Pallas kernels  241 us (88%)
  other arithmetic  15.3 us (6%)
  between operations  8.3 us (3%)
  local copies, waits for them, and re-layouts  7.86 us (3%)
    pallas_call x2, Pallas kernels, sweep(): pl.pallas_call(functools.partial(sweep_kernel, first), out_shape=(jax.Sha...  135 us
    pallas_call x3, Pallas kernels, gather_small(): pl.pallas_call(gather_small_kernel, out_shape=jax.ShapeDtypeStruct((rows,...  36.2 us
    pallas_call x1, Pallas kernels, exchange_blocks(): pl.pallas_call(functools.partial(exchange_kernel, x.shape[0] // n), out_s...  30.4 us
    pallas_call x2, Pallas kernels, apply_blocks(): pl.pallas_call(functools.partial(apply_kernel, first), out_shape=(jax.Sha...  20.9 us
    sub x1, other arithmetic, on_device(): residual = targets.astype(F32) - mixed * image0 - alpha1 * image1  8.61 us
    pallas_call x1, Pallas kernels, next_terms(): pl.pallas_call(next_terms_kernel, out_shape=jax.ShapeDtypeStruct((x.shape...  8.52 us
    pallas_call x1, Pallas kernels, first_terms(): pl.pallas_call(first_terms_kernel, out_shape=jax.ShapeDtypeStruct((x.shap...  6.45 us

commit v1 on v0

v1 whole, which is shorter than its diff:
```python
import functools

import jax
import jax.numpy as jnp
from jax import lax
from jax.experimental import pallas as pl
from jax.experimental.pallas import tpu as pltpu
from jax.sharding import PartitionSpec as P

BLOCK = 128
T_STEPS = 64
RIDGE_SHARE = 0.2
LANES = 128
SIZE = 3
LEAD = 4
FAR = 6
LATE = 2
VMEM = pltpu.VMEM
F32 = jnp.float32
BF16 = jnp.bfloat16
WHOLE = pl.BlockSpec(memory_space=pltpu.VMEM)
SCALARS = pl.BlockSpec(memory_space=pltpu.SMEM)
MESH = pl.DeviceIdType.MESH


def enter(axes):
    barrier = pltpu.get_barrier_semaphore()
    count = 0
    for axis in axes:
        n = lax.axis_size(axis)
        me = lax.axis_index(axis)
        for k in range(1, n):
            pl.semaphore_signal(
                barrier, inc=1, device_id={axis: lax.rem(me + k, n)}, device_id_type=MESH,
            )
        count += n - 1
    pl.semaphore_wait(barrier, count)


def push(src, dst, send, recv, axis, k):
    n = lax.axis_size(axis)
    return pltpu.make_async_remote_copy(
        src_ref=src, dst_ref=dst, send_sem=send, recv_sem=recv,
        device_id={axis: lax.rem(lax.axis_index(axis) + k, n)},
        device_id_type=MESH,
    )


def gather_small_kernel(x_ref, out_ref, send_c, recv_c, send_r, recv_r):
    cols, rows = lax.axis_size("col"), lax.axis_size("row")
    my_col, my_row = lax.axis_index("col"), lax.axis_index("row")
    enter(("col", "row"))
    out_ref[my_row, my_col] = x_ref[...]
    first = [
        push(x_ref, out_ref.at[my_row, my_col], send_c.at[k - 1], recv_c.at[k - 1], "col", k)
        for k in range(1, cols)
    ]
    for copy in first:
        copy.start()
    for copy in first:
        copy.wait()
    second = [
        push(out_ref.at[my_row], out_ref.at[my_row], send_r.at[k - 1], recv_r.at[k - 1], "row", k)
        for k in range(1, rows)
    ]
    for copy in second:
        copy.start()
    for copy in second:
        copy.wait()


def gather_small(x, call_id):
    cols, rows = lax.axis_size("col"), lax.axis_size("row")
    return pl.pallas_call(
        gather_small_kernel,
        out_shape=jax.ShapeDtypeStruct((rows, cols) + x.shape, x.dtype),
        in_specs=[WHOLE],
        out_specs=WHOLE,
        scratch_shapes=[
            pltpu.SemaphoreType.DMA((cols - 1,)), pltpu.SemaphoreType.DMA((cols - 1,)),
            pltpu.SemaphoreType.DMA((rows - 1,)), pltpu.SemaphoreType.DMA((rows - 1,)),
        ],
        compiler_params=pltpu.CompilerParams(collective_id=call_id, has_side_effects=True),
    )(x)


def block_dot(x, e):
    return lax.dot_general(x, e, (((0,), (0,)), ((), ())), preferred_element_type=F32)


def fold(values):
    return jnp.sum(values.reshape(values.shape[0] // 8, 8, BLOCK), axis=0)


def xor(a, b, bits):
    out = 0
    for i in range(bits):
        x = lax.rem(lax.div(a, 2 ** i), 2)
        if isinstance(b, int):
            y = (b >> i) & 1
        else:
            y = lax.rem(lax.div(b, 2 ** i), 2)
        out = out + (x + y - 2 * x * y) * 2 ** i
    return out


def fit_kernel(
    run, ridge, index_ref, ends_ref, x_ref, t_ref, w_ref, image_ref, coeffs_ref,
    give, x_all, near_sum, far_sum, arrived, d_ref, low_ref, s_ref, acc, scal, mine, by_col, line, by_row,
    send_x, recv_x, send_z, recv_z, send_c, recv_c, send_r, recv_r, credit,
):
    cols, rows = lax.axis_size("col"), lax.axis_size("row")
    my_col, my_row = lax.axis_index("col"), lax.axis_index("row")
    bits = (cols - 1).bit_length()
    count = x_all.shape[0]
    pieces = count // SIZE
    per_run = run // SIZE
    enter(("col", "row"))

    def select(s, target):
        base = xor(my_col, s, bits) * run

        def one(i, carry):
            column = index_ref[0, base + i] * BLOCK
            target[s * run + i] = x_ref[:, pl.ds(column, BLOCK)]
            return carry

        lax.fori_loop(0, run, one, 0, unroll=3)

    def exchange(s):
        place = pl.ds(s * run, run)
        return pltpu.make_async_remote_copy(
            src_ref=give.at[place], dst_ref=x_all.at[place],
            send_sem=send_x.at[s - 1], recv_sem=recv_x.at[s - 1],
            device_id={"col": xor(my_col, s, bits)}, device_id_type=MESH,
        )

    for s in range(1, cols):
        select(s, give)
        exchange(s).start()
    select(0, x_all)

    near = lax.div(2 * my_row, rows)
    far = 1 - near
    has_near = jnp.logical_and(my_row > 0, my_row < rows - 1)
    at_end = (my_row == 0) | (my_row == rows - 1)
    to_far = my_row + 1 - 2 * near
    to_near = my_row - 1 + 2 * near

    def forth(p):
        place = pl.ds(p * SIZE, SIZE)
        return pltpu.make_async_remote_copy(
            src_ref=near_sum.at[place], dst_ref=arrived.at[near, place],
            send_sem=send_z.at[near, p], recv_sem=recv_z.at[near, p],
            device_id={"row": to_far}, device_id_type=MESH,
        )

    def back(p):
        place = pl.ds(p * SIZE, SIZE)
        return pltpu.make_async_remote_copy(
            src_ref=far_sum.at[place], dst_ref=arrived.at[far, place],
            send_sem=send_z.at[far, p], recv_sem=recv_z.at[far, p],
            device_id={"row": to_near}, device_id_type=MESH,
        )

    def listed(p):
        s = lax.div(p, per_run)
        return xor(my_col, s, bits) * run + (p - s * per_run) * SIZE

    def store_terms(p, terms):
        for j in range(SIZE):
            near_sum[p * SIZE + j] = terms[j]
            far_sum[p * SIZE + j] = terms[j]
        pl.when(at_end)(lambda: forth(p).start())

    def pass_forth(p):
        forth(p).wait_recv()
        for j in range(SIZE):
            b = p * SIZE + j
            near_sum[b] = (far_sum[b].astype(F32) + arrived[near, b].astype(F32)).astype(BF16)
        forth(p).start()

    def pass_back(p):
        back(p).wait_recv()

        @pl.when(has_near)
        def _():
            for j in range(SIZE):
                b = p * SIZE + j
                far_sum[b] = (far_sum[b].astype(F32) + arrived[far, b].astype(F32)).astype(BF16)
            back(p).start()

    def sweep(make, settle, hooks, last):
        def body(q, carry):
            pl.when(q < pieces)(lambda: make(q))
            pl.when(has_near & (q >= LEAD) & (q < pieces + LEAD))(lambda: pass_forth(q - LEAD))
            pl.when((q >= FAR) & (q < pieces + FAR))(lambda: pass_back(q - FAR))
            for when, hook in hooks:
                pl.when(q == when)(hook)
            pl.when(q >= last)(lambda: settle(q - last))
            return carry

        lax.fori_loop(0, pieces + last, body, 0)

        def drain(p, carry):
            forth(p).wait_send()
            pl.when(has_near)(lambda: back(p).wait_send())
            return carry

        lax.fori_loop(0, pieces, drain, 0)

    def over_col(a, k):
        return push(mine.at[a], by_col.at[a, my_col], send_c.at[a, k - 1], recv_c.at[a, k - 1], "col", k)

    def over_row(a, k):
        return push(line.at[a], by_row.at[a, my_row], send_r.at[a, k - 1], recv_r.at[a, k - 1], "row", k)

    def reduce_start(a, wanted):
        tile = jnp.concatenate(
            [jnp.sum(acc[j], axis=0, keepdims=True) for j in wanted]
            + [jnp.zeros((8 - len(wanted), LANES), F32)], axis=0,
        )
        mine[a] = tile
        by_col[a, my_col] = tile
        for k in range(1, cols):
            over_col(a, k).start()

    def reduce_middle(a):
        for k in range(1, cols):
            over_col(a, k).wait()
        tile = by_col[a, 0]
        for j in range(1, cols):
            tile = tile + by_col[a, j]
        line[a] = tile
        by_row[a, my_row] = tile
        for k in range(1, rows):
            over_row(a, k).start()

    def reduce_end(a):
        for k in range(1, rows):
            over_row(a, k).wait()
        tile = by_row[a, 0]
        for j in range(1, rows):
            tile = tile + by_row[a, j]
        return jnp.sum(tile, axis=1, keepdims=True)

    def wide(value):
        return jnp.broadcast_to(value, (1, LANES))

    acc[...] = jnp.zeros_like(acc)
    s_ref[count] = jnp.zeros((BLOCK, BLOCK), F32)
    image_ref[count] = jnp.zeros((BLOCK, BLOCK), F32)

    def first_make(p):
        s = lax.div(p, per_run)

        @pl.when((s > 0) & (s * per_run == p))
        def _():
            place = pl.ds(s * run, run)
            pltpu.make_async_remote_copy(
                src_ref=give.at[place], dst_ref=x_all.at[place],
                send_sem=send_x.at[s - 1], recv_sem=recv_x.at[s - 1],
                device_id={"col": xor(my_col, s, bits)}, device_id_type=MESH,
            ).wait_recv()

        base = listed(p)
        terms = []
        for j in range(SIZE):
            place = pl.ds(index_ref[1, base + j] * BLOCK, BLOCK)
            e = (t_ref[:, place].astype(F32) * w_ref[...]).astype(BF16)
            terms.append(block_dot(x_all[p * SIZE + j], e).astype(BF16))
        store_terms(p, terms)

    def first_settle(p):
        base = listed(p)
        made = []
        for j in range(SIZE):
            b = p * SIZE + j
            total = near_sum[b].astype(F32) + arrived[far, b].astype(F32)
            rounded = total.astype(BF16)
            flat = rounded.astype(F32)
            d_ref[b] = rounded
            low_ref[b] = (total - flat).astype(BF16)
            made.append(jnp.dot(x_all[b], rounded, preferred_element_type=F32))
            acc[0] += fold(total * total)
            acc[1] += fold(flat * flat)
        for j in range(SIZE):
            b = p * SIZE + j
            image = made[j] + s_ref[index_ref[2, base + j]]
            s_ref[b] = image
            acc[2] += ends_ref[base + j] * fold(w_ref[...] * image * image)

    sweep(first_make, first_settle, [], FAR)
    for s in range(1, cols):
        exchange(s).wait_send()

    def greet(other):
        pl.semaphore_signal(credit, inc=1, device_id={"row": other}, device_id_type=MESH)

    has_left, has_right = my_row > 0, my_row < rows - 1
    pl.when(has_left)(lambda: greet(my_row - 1))
    pl.when(has_right)(lambda: greet(my_row + 1))
    reduce_start(0, (0, 1, 2))
    pl.semaphore_wait(credit, has_left.astype(jnp.int32) + has_right.astype(jnp.int32))

    share = 1.0 / rows

    def first_scalars():
        total = reduce_end(0)
        gamma, flat, square = total[0:1] * share, total[1:2] * share, total[2:3]
        alpha = gamma / (square + ridge * flat)
        scal[0:1] = wide(alpha)
        scal[1:2] = wide(ridge * alpha)
        scal[2:3] = wide(gamma)
        scal[3:4] = wide(flat)
        scal[4:5] = wide(square)

    def second_make(p):
        base = listed(p)
        terms = []
        for j in range(SIZE):
            e = (s_ref[index_ref[3, base + j]] * w_ref[...]).astype(BF16)
            terms.append(block_dot(x_all[p * SIZE + j], e).astype(BF16))
        store_terms(p, terms)

    def second_settle(p):
        base = listed(p)
        alpha, shift = scal[0:1], scal[1:2]
        made = []
        for j in range(SIZE):
            b = p * SIZE + j
            total = near_sum[b].astype(F32) + arrived[far, b].astype(F32)
            flat = d_ref[b].astype(F32)
            gradient = flat + low_ref[b].astype(F32) - alpha * total - shift * flat
            rounded = gradient.astype(BF16)
            low_ref[b] = rounded
            step = rounded.astype(F32)
            made.append(jnp.dot(x_all[b], rounded, preferred_element_type=F32))
            acc[3] += fold(gradient * gradient)
            acc[4] += fold(step * step)
            acc[5] += fold(step * flat)
        for j in range(SIZE):
            b = p * SIZE + j
            image = made[j] + image_ref[index_ref[2, base + j]]
            image_ref[b] = image
            final = ends_ref[base + j]
            weighted = w_ref[...] * image
            acc[6] += final * fold(weighted * image)
            acc[7] += final * fold(weighted * s_ref[b])

    last = FAR + LATE
    sweep(second_make, second_settle,
          [(LEAD - 1, lambda: reduce_middle(0)), (last, first_scalars)], last)

    reduce_start(1, (3, 4, 5, 6, 7))
    reduce_middle(1)
    total = reduce_end(1)
    alpha, gamma = scal[0:1], scal[2:3]
    flat, square = scal[3:4], scal[4:5]
    gamma_next = wide(total[0:1]) * share
    beta = gamma_next / gamma
    flat_next = wide(total[1:2]) * share + 2.0 * beta * wide(total[2:3]) * share + beta * beta * flat
    square_next = wide(total[3:4]) + 2.0 * beta * wide(total[4:5]) + beta * beta * square
    alpha_next = gamma_next / (square_next + ridge * flat_next)
    mixed = alpha + alpha_next * beta

    def mix(b, carry):
        image_ref[b] = mixed * s_ref[b] + alpha_next * image_ref[b]
        return carry

    lax.fori_loop(0, count, mix, 0, unroll=2)

    runs = coeffs_ref.shape[0] // run
    for u in range(runs):
        slot = xor(my_col, my_row * runs + u, bits)

        def own(i, carry):
            b = slot * run + i
            coeffs_ref[u * run + i] = mixed * d_ref[b].astype(F32) + alpha_next * low_ref[b].astype(F32)
            return carry

        lax.fori_loop(0, run, own, 0)


def fit(index, ends, x, targets, weight, run, ridge, shard):
    cols, rows = lax.axis_size("col"), lax.axis_size("row")
    count = run * cols
    samples = x.shape[0]
    pieces = count // SIZE
    block = (BLOCK, BLOCK)
    dma = pltpu.SemaphoreType.DMA
    return pl.pallas_call(
        functools.partial(fit_kernel, run, ridge),
        out_shape=(
            jax.ShapeDtypeStruct((count + 1, samples, BLOCK), F32),
            jax.ShapeDtypeStruct((shard,) + block, F32),
        ),
        in_specs=[SCALARS, SCALARS, WHOLE, WHOLE, WHOLE],
        out_specs=(WHOLE, WHOLE),
        scratch_shapes=[
            VMEM((count, samples, BLOCK), BF16), VMEM((count, samples, BLOCK), BF16),
            VMEM((count,) + block, BF16), VMEM((count,) + block, BF16),
            VMEM((2, count) + block, BF16),
            VMEM((count,) + block, BF16), VMEM((count,) + block, BF16),
            VMEM((count + 1, samples, BLOCK), F32),
            VMEM((8, 8, LANES), F32), VMEM((8, LANES), F32),
            VMEM((2, 8, LANES), F32), VMEM((2, cols, 8, LANES), F32),
            VMEM((2, 8, LANES), F32), VMEM((2, rows, 8, LANES), F32),
            dma((cols - 1,)), dma((cols - 1,)),
            dma((2, pieces)), dma((2, pieces)),
            dma((2, cols - 1)), dma((2, cols - 1)),
            dma((2, rows - 1)), dma((2, rows - 1)),
            pltpu.SemaphoreType.REGULAR,
        ],
        compiler_params=pltpu.CompilerParams(
            collective_id=2, has_side_effects=True, vmem_limit_bytes=66_000_000,
        ),
    )(index, ends, x, targets, weight)


def spread_kernel(index_ref, t_ref, image_ref, out_ref):
    def one(c, carry):
        place = pl.ds(pl.multiple_of(c * BLOCK, BLOCK), BLOCK)
        out_ref[:, place] = t_ref[:, place].astype(F32) - image_ref[index_ref[c]]
        return carry

    lax.fori_loop(0, index_ref.shape[0], one, 0, unroll=2)


def spread(index, targets, image):
    return pl.pallas_call(
        spread_kernel,
        out_shape=jax.ShapeDtypeStruct(targets.shape, F32),
        in_specs=[SCALARS, WHOLE, WHOLE],
        out_specs=WHOLE,
    )(index, targets, image)


def on_device(samples_x, targets, times, block_rows, block_cols):
    col_count = lax.axis_size("col")
    row_count = lax.axis_size("row")
    taxa_col = samples_x.shape[1]
    sample_count = samples_x.shape[0]
    column_count = taxa_col // BLOCK
    my_col = lax.axis_index("col")
    shard = block_rows.shape[0]
    count = shard * row_count
    run = count // col_count
    ridge = RIDGE_SHARE * sample_count * row_count
    weight = jnp.broadcast_to(
        (0.5 + times.astype(F32) / T_STEPS)[:, None], (sample_count, BLOCK)
    )
    places = jnp.pad(
        jnp.stack([block_rows, block_cols]), ((0, 6), (0, LANES - shard))
    )
    everywhere = gather_small(places, 1)
    rows_all = everywhere[:, :, 0, :shard].transpose(1, 0, 2).reshape(col_count, count)
    wanted = lax.dynamic_slice_in_dim(rows_all, my_col * run, run, 1) - my_col * column_count
    cols_mine = lax.dynamic_index_in_dim(everywhere[:, :, 1, :shard], my_col, 1, keepdims=False)
    cols = cols_mine.reshape(count) - my_col * column_count

    number = lax.iota(jnp.int32, count)
    slot = jnp.bitwise_xor(lax.div(number, run), my_col) * run + lax.rem(number, run)
    same = cols[:, None] == cols[None, :]
    final = jnp.max(jnp.where(same, slot[None, :], -1), axis=1)
    before = jnp.max(jnp.where(same & (slot[None, :] < slot[:, None]), slot[None, :], -1), axis=1)
    before = jnp.where(before < 0, count, before)
    held = lax.iota(jnp.int32, column_count)[:, None] == cols[None, :]
    end = jnp.max(jnp.where(held, slot[None, :], -1), axis=1)
    end = jnp.where(end < 0, count, end)
    index = jnp.stack([wanted.reshape(count), cols, before, final])

    image, coeffs = fit(index, (final == slot).astype(F32), samples_x, targets, weight, run, ridge, shard)
    return (coeffs, spread(end, targets, image))


def solution(mesh):
    placed = (P("row", "col"), P("row", "col"), P("row"), P(("col", "row")), P(("col", "row")))
    return jax.shard_map(
        on_device,
        mesh=mesh,
        in_specs=placed,
        out_specs=(P(("col", "row"), None, None), P("row", "col")),
        check_vma=False,
    )
```

time: 273 us -> 173 us (0.63)
  Pallas kernels: 241 us -> 164 us
  other arithmetic: 15.3 us -> 4.1 us
  between operations: 8.3 us -> 0.69 us
  local copies, waits for them, and re-layouts: 7.86 us -> 4.17 us
    pallas_call x8 -> x2, Pallas kernels: 205 us -> 149 us  [the longest x1 141 us: fit(): pl.pallas_call(functools.partial(fit_kernel, run, ridge), out_shape=(jax....]
    pallas_call x3 -> x1, Pallas kernels: 36.2 us -> 14.4 us  [gather_small(): pl.pallas_call(gather_small_kernel, out_shape=jax.ShapeDtypeStruct((rows,...]
    sub x2 -> x1, other arithmetic: 8.64 us -> 0.67 us  [on_device(): cols = cols_mine.reshape(count) - my_col * column_count]
    slice x7 -> x1, local copies, waits for them, and re-layouts: 5.02 us -> 1.01 us  [on_device(): everywhere[:, :, 0, :shard].transpose(1, 0, 2).reshape(col_count, count)]
where the time goes in v1:
time: 173 us
  Pallas kernels  164 us (95%)
  local copies, waits for them, and re-layouts  4.17 us (2%)
  other arithmetic  4.1 us (2%)
    pallas_call x1, Pallas kernels, fit(): pl.pallas_call(functools.partial(fit_kernel, run, ridge), out_shape=(jax....  141 us
    pallas_call x1, Pallas kernels, gather_small(): pl.pallas_call(gather_small_kernel, out_shape=jax.ShapeDtypeStruct((rows,...  14.4 us
    pallas_call x1, Pallas kernels, spread(): pl.pallas_call(spread_kernel, out_shape=jax.ShapeDtypeStruct(targets.shap...  7.7 us

profile of v1, /device:TPU:0, one launch (start us, length us, event | category | flops | bytes accessed | tf_op | source)
XLA Modules:
  0.0 172.6 jit_solution(2172810110757256937)
XLA Ops:
  0.6 0.7 multiply_add_fusion
  1.3 0.7 pad_add_fusion.1
  2.0 0.6 pad.4.x_ref
  2.6 0.7 broadcast_in_dim.51.w_ref
  3.3 14.4 %shard_map.68 = s32[4,8,8,128]{3,2,1,0:T(8,128)} custom-call(s32[8,128]{1,0:T(8,128)} %pad.4.x_ref), custom_call_target="tpu_custom_call" | custom-call | tf_op jit(solution)/shard_map/pallas_call | solution.py:74
  17.7 1.0 fusion.2
  18.8 0.1 reshape.60
  18.8 0.1 dynamic-slice_subtract_fusion
  18.9 0.5 broadcast.78
  19.4 0.7 fusion.1
  20.1 0.1 stack_reshape.3
  20.2 0.1 sub.34
  20.3 0.1 sub.35
  20.3 0.1 select_reduce_fusion
  20.5 0.6 compare_select_fusion.1.index_ref
  21.1 0.2 select_reduce_fusion.1
  21.2 0.5 compare_convert_fusion.ends_ref
  21.8 0.6 pad_add_fusion.index_ref
  22.4 141.5 %shard_map.69 = (f32[73,128,128]{2,1,0:T(8,128)}, f32[18,128,128]{2,1,0:T(8,128)}) custom-call(s32[4,72]{1,0:T(4,128)} %pad_add_fusion.index_ref, f32[72]{0:T(128)} %compare_convert_fusion.ends_ref, bf16[128,12288]{1,0:T(8,128)(2,1)} %x_ref.1, bf16[128,12288]{1,0:T(8,128)(2,1)} %t_ref.3, f32[128,128]{1,0:T(8,128)} %broadcast_in_dim.51.w_ref), custom_call_target="tpu_custom_call" | custom-call | tf_op jit(solution)/shard_map/pallas_call | solution.py:392
  163.8 0.0 copy-start
  163.9 7.7 %shard_map.70 = f32[128,12288]{1,0:T(8,128)} custom-call(s32[96]{0:T(128)} %compare_select_fusion.1.index_ref, bf16[128,12288]{1,0:T(8,128)(2,1)} %t_ref.3, f32[73,128,128]{2,1,0:T(8,128)} %get-tuple-element.5.image_ref), custom_call_target="tpu_custom_call" | custom-call | tf_op jit(solution)/shard_map/pallas_call | solution.py:431
  171.6 0.0 copy-done
  171.6 1.0 copy.10
  (3 shorter events, 0.0 us)
Async XLA Ops:
  163.8 7.7 %copy-start = (f32[18,128,128]{2,1,0:T(8,128)S(1)}, f32[18,128,128]{2,1,0:T(8,128)}, u32[]{:S(2)}) copy-start(f32[18,128,128]{2,1,0:T(8,128)} %get-tuple-element.14) | copy-start | bytes 3538948

commit v2 on v1

--- a/solution.py
+++ b/solution.py
@@ -14,12 +14,14 @@
 SIZE = 3
 LEAD = 4
 FAR = 6
-LATE = 2
+LATE = 1
+STEPS = 4
 VMEM = pltpu.VMEM
 F32 = jnp.float32
 BF16 = jnp.bfloat16
 WHOLE = pl.BlockSpec(memory_space=pltpu.VMEM)
 SCALARS = pl.BlockSpec(memory_space=pltpu.SMEM)
+APART = pl.BlockSpec(memory_space=pl.ANY)
 MESH = pl.DeviceIdType.MESH
 
 
@@ -46,42 +48,98 @@
     )
 
 
-def gather_small_kernel(x_ref, out_ref, send_c, recv_c, send_r, recv_r):
+def positions_kernel(taken, rows_ref, cols_ref, row_out, col_out, tile, by_col, by_row, send_a, recv_a, send_b, recv_b):
     cols, rows = lax.axis_size("col"), lax.axis_size("row")
     my_col, my_row = lax.axis_index("col"), lax.axis_index("row")
-    enter(("col", "row"))
-    out_ref[my_row, my_col] = x_ref[...]
-    first = [
-        push(x_ref, out_ref.at[my_row, my_col], send_c.at[k - 1], recv_c.at[k - 1], "col", k)
-        for k in range(1, cols)
-    ]
-    for copy in first:
-        copy.start()
-    for copy in first:
-        copy.wait()
-    second = [
-        push(out_ref.at[my_row], out_ref.at[my_row], send_r.at[k - 1], recv_r.at[k - 1], "row", k)
-        for k in range(1, rows)
-    ]
-    for copy in second:
-        copy.start()
-    for copy in second:
-        copy.wait()
-
-
-def gather_small(x, call_id):
+    ratio = cols // rows
+    source = lax.div(my_col, ratio)
+    alone = source == my_row
+    barrier = pltpu.get_barrier_semaphore()
+
+    def greet(col, row):
+        pl.semaphore_signal(barrier, inc=1, device_id={"col": col, "row": row}, device_id_type=MESH)
+
+    greet_self = jnp.where(alone, 1, 0)
+    for k in range(1, cols):
+        greet(lax.rem(my_col + k, cols), source)
+    pl.when(source != my_row)(lambda: greet(my_col, source))
+    for k in range(1, rows):
+        greet(my_col, lax.rem(my_row + k, rows))
+    shard = rows_ref.shape[1]
+    tile[...] = jnp.zeros_like(tile)
+    tile[0:1, 0:shard] = rows_ref[...]
+    tile[1:2, 0:shard] = cols_ref[...]
+    pl.semaphore_wait(barrier, ratio * rows - greet_self + rows - 1)
+
+    def to_reader(j, row, k):
+        return pltpu.make_async_remote_copy(
+            src_ref=tile, dst_ref=by_col.at[my_col], send_sem=send_a.at[k], recv_sem=recv_a.at[my_col],
+            device_id={"col": my_row * ratio + j, "row": row}, device_id_type=MESH,
+        )
+
+    def to_group(k):
+        return pltpu.make_async_remote_copy(
+            src_ref=tile, dst_ref=by_row.at[my_row], send_sem=send_b.at[k], recv_sem=recv_b.at[my_row],
+            device_id={"row": lax.rem(my_row + k, rows)}, device_id_type=MESH,
+        )
+
+    def each(act):
+        for j in range(ratio):
+            for row in range(rows):
+                other = (my_row * ratio + j != my_col) | (my_row != row)
+                pl.when(other)(lambda j=j, row=row: act(to_reader(j, row, j * rows + row)))
+
+    each(lambda copy: copy.start())
+    for k in range(1, rows):
+        to_group(k).start()
+    by_row[my_row] = tile[...]
+
+    @pl.when(alone)
+    def _():
+        by_col[my_col] = tile[...]
+
+    def from_col(col):
+        return pltpu.make_async_remote_copy(
+            src_ref=tile, dst_ref=by_col.at[col], send_sem=send_a.at[0], recv_sem=recv_a.at[col],
+            device_id={"col": col, "row": source}, device_id_type=MESH,
+        )
+
+    def from_row(row):
+        return pltpu.make_async_remote_copy(
+            src_ref=tile, dst_ref=by_row.at[row], send_sem=send_b.at[0], recv_sem=recv_b.at[row],
+            device_id={"row": row}, device_id_type=MESH,
+        )
+
+    for k in range(1, cols):
+        from_col(lax.rem(my_col + k, cols)).wait_recv()
+    pl.when(source != my_row)(lambda: from_col(my_col).wait_recv())
+    for k in range(1, rows):
+        from_row(lax.rem(my_row + k, rows)).wait_recv()
+    for col in range(cols):
+        row_out[col:col + 1, :] = by_col[col, 0:1, :] - my_col * taken
+    for row in range(rows):
+        col_out[row:row + 1, :] = by_row[row, 1:2, :] - my_col * taken
+    each(lambda copy: copy.wait_send())
+    for k in range(1, rows):
+        to_group(k).wait_send()
+
+
+def positions(block_rows, block_cols, taken, call_id):
     cols, rows = lax.axis_size("col"), lax.axis_size("row")
+    dma = pltpu.SemaphoreType.DMA
     return pl.pallas_call(
-        gather_small_kernel,
-        out_shape=jax.ShapeDtypeStruct((rows, cols) + x.shape, x.dtype),
-        in_specs=[WHOLE],
-        out_specs=WHOLE,
+        functools.partial(positions_kernel, taken),
+        out_shape=(
+            jax.ShapeDtypeStruct((cols, LANES), jnp.int32), jax.ShapeDtypeStruct((rows, LANES), jnp.int32),
+        ),
+        in_specs=[WHOLE, WHOLE],
+        out_specs=(WHOLE, WHOLE),
         scratch_shapes=[
-            pltpu.SemaphoreType.DMA((cols - 1,)), pltpu.SemaphoreType.DMA((cols - 1,)),
-            pltpu.SemaphoreType.DMA((rows - 1,)), pltpu.SemaphoreType.DMA((rows - 1,)),
+            VMEM((8, LANES), jnp.int32), VMEM((cols, 8, LANES), jnp.int32), VMEM((rows, 8, LANES), jnp.int32),
+            dma((cols,)), dma((cols,)), dma((rows,)), dma((rows,)),
         ],
         compiler_params=pltpu.CompilerParams(collective_id=call_id, has_side_effects=True),
-    )(x)
+    )(block_rows[None], block_cols[None])
 
 
 def block_dot(x, e):
@@ -105,9 +163,9 @@
 
 
 def fit_kernel(
-    run, ridge, index_ref, ends_ref, x_ref, t_ref, w_ref, image_ref, coeffs_ref,
-    give, x_all, near_sum, far_sum, arrived, d_ref, low_ref, s_ref, acc, scal, mine, by_col, line, by_row,
-    send_x, recv_x, send_z, recv_z, send_c, recv_c, send_r, recv_r, credit,
+    run, ridge, row_ref, col_ref, index_ref, ends_ref, times_ref, x_hbm, t_hbm, image_hbm, coeffs_ref,
+    x_ref, t_ref, w_ref, image_ref, give, x_all, near_sum, far_sum, arrived, d_ref, low_ref, s_ref, acc, scal, mine, by_col, line, by_row,
+    send_x, recv_x, send_z, recv_z, send_c, recv_c, send_r, recv_r, credit, load, leave,
 ):
     cols, rows = lax.axis_size("col"), lax.axis_size("row")
     my_col, my_row = lax.axis_index("col"), lax.axis_index("row")
@@ -115,13 +173,25 @@
     count = x_all.shape[0]
     pieces = count // SIZE
     per_run = run // SIZE
+    shard = coeffs_ref.shape[0]
+    load_x = pltpu.make_async_copy(x_hbm, x_ref, load.at[0])
+    load_t = pltpu.make_async_copy(t_hbm, t_ref, load.at[1])
+    load_x.start()
+    load_t.start()
+    weight = 0.5 + times_ref[...].astype(F32) / T_STEPS
+    w_ref[...] = jnp.transpose(jnp.broadcast_to(weight, (BLOCK, weight.shape[1])))
+    acc[...] = jnp.zeros_like(acc)
+    s_ref[count] = jnp.zeros((BLOCK, BLOCK), F32)
+    image_ref[count] = jnp.zeros((BLOCK, BLOCK), F32)
     enter(("col", "row"))
+    load_x.wait()
 
     def select(s, target):
-        base = xor(my_col, s, bits) * run
+        group = xor(my_col, s, bits)
+        base = lax.rem(my_col, shard // run) * run
 
         def one(i, carry):
-            column = index_ref[0, base + i] * BLOCK
+            column = row_ref[group, base + i] * BLOCK
             target[s * run + i] = x_ref[:, pl.ds(column, BLOCK)]
             return carry
 
@@ -135,10 +205,15 @@
             device_id={"col": xor(my_col, s, bits)}, device_id_type=MESH,
         )
 
-    for s in range(1, cols):
+    def offer(s):
         select(s, give)
         exchange(s).start()
+
     select(0, x_all)
+    for s in range(1, min(4, cols)):
+        offer(s)
+    later = [(s - 4, functools.partial(offer, s)) for s in range(4, cols)]
+    load_t.wait()
 
     near = lax.div(2 * my_row, rows)
     far = 1 - near
@@ -247,10 +322,6 @@
     def wide(value):
         return jnp.broadcast_to(value, (1, LANES))
 
-    acc[...] = jnp.zeros_like(acc)
-    s_ref[count] = jnp.zeros((BLOCK, BLOCK), F32)
-    image_ref[count] = jnp.zeros((BLOCK, BLOCK), F32)
-
     def first_make(p):
         s = lax.div(p, per_run)
 
@@ -266,7 +337,8 @@
         base = listed(p)
         terms = []
         for j in range(SIZE):
-            place = pl.ds(index_ref[1, base + j] * BLOCK, BLOCK)
+            column = col_ref[lax.div(base + j, shard), lax.rem(base + j, shard)]
+            place = pl.ds(column * BLOCK, BLOCK)
             e = (t_ref[:, place].astype(F32) * w_ref[...]).astype(BF16)
             terms.append(block_dot(x_all[p * SIZE + j], e).astype(BF16))
         store_terms(p, terms)
@@ -286,11 +358,11 @@
             acc[1] += fold(flat * flat)
         for j in range(SIZE):
             b = p * SIZE + j
-            image = made[j] + s_ref[index_ref[2, base + j]]
+            image = made[j] + s_ref[index_ref[0, base + j]]
             s_ref[b] = image
             acc[2] += ends_ref[base + j] * fold(w_ref[...] * image * image)
 
-    sweep(first_make, first_settle, [], FAR)
+    sweep(first_make, first_settle, later, FAR)
     for s in range(1, cols):
         exchange(s).wait_send()
 
@@ -319,7 +391,7 @@
         base = listed(p)
         terms = []
         for j in range(SIZE):
-            e = (s_ref[index_ref[3, base + j]] * w_ref[...]).astype(BF16)
+            e = (s_ref[index_ref[1, base + j]] * w_ref[...]).astype(BF16)
             terms.append(block_dot(x_all[p * SIZE + j], e).astype(BF16))
         store_terms(p, terms)
 
@@ -341,7 +413,7 @@
             acc[5] += fold(step * flat)
         for j in range(SIZE):
             b = p * SIZE + j
-            image = made[j] + image_ref[index_ref[2, base + j]]
+            image = made[j] + image_ref[index_ref[0, base + j]]
             image_ref[b] = image
             final = ends_ref[base + j]
             weighted = w_ref[...] * image
@@ -364,11 +436,18 @@
     alpha_next = gamma_next / (square_next + ridge * flat_next)
     mixed = alpha + alpha_next * beta
 
-    def mix(b, carry):
-        image_ref[b] = mixed * s_ref[b] + alpha_next * image_ref[b]
-        return carry
-
-    lax.fori_loop(0, count, mix, 0, unroll=2)
+    def leaving(s):
+        place = pl.ds(s * run, run)
+        return pltpu.make_async_copy(give.at[place], image_hbm.at[place], leave.at[s])
+
+    for s in range(cols):
+        def mix(i, carry):
+            b = s * run + i
+            give[b] = (mixed * s_ref[b] + alpha_next * image_ref[b]).astype(BF16)
+            return carry
+
+        lax.fori_loop(0, run, mix, 0, unroll=3)
+        leaving(s).start()
 
     runs = coeffs_ref.shape[0] // run
     for u in range(runs):
@@ -380,9 +459,11 @@
             return carry
 
         lax.fori_loop(0, run, own, 0)
-
-
-def fit(index, ends, x, targets, weight, run, ridge, shard):
+    for s in range(cols):
+        leaving(s).wait()
+
+
+def fit(row_places, col_places, index, ends, times, x, targets, run, ridge, shard):
     cols, rows = lax.axis_size("col"), lax.axis_size("row")
     count = run * cols
     samples = x.shape[0]
@@ -392,12 +473,14 @@
     return pl.pallas_call(
         functools.partial(fit_kernel, run, ridge),
         out_shape=(
-            jax.ShapeDtypeStruct((count + 1, samples, BLOCK), F32),
+            jax.ShapeDtypeStruct((count, samples, BLOCK), BF16),
             jax.ShapeDtypeStruct((shard,) + block, F32),
         ),
-        in_specs=[SCALARS, SCALARS, WHOLE, WHOLE, WHOLE],
-        out_specs=(WHOLE, WHOLE),
+        in_specs=[SCALARS, SCALARS, SCALARS, SCALARS, WHOLE, APART, APART],
+        out_specs=(APART, WHOLE),
         scratch_shapes=[
+            VMEM(x.shape, BF16), VMEM(x.shape, BF16), VMEM((samples, BLOCK), F32),
+            VMEM((count + 1, samples, BLOCK), F32),
             VMEM((count, samples, BLOCK), BF16), VMEM((count, samples, BLOCK), BF16),
             VMEM((count,) + block, BF16), VMEM((count,) + block, BF16),
             VMEM((2, count) + block, BF16),
@@ -410,29 +493,38 @@
             dma((2, pieces)), dma((2, pieces)),
             dma((2, cols - 1)), dma((2, cols - 1)),
             dma((2, rows - 1)), dma((2, rows - 1)),
-            pltpu.SemaphoreType.REGULAR,
+            pltpu.SemaphoreType.REGULAR, dma((2,)), dma((cols,)),
         ],
         compiler_params=pltpu.CompilerParams(
             collective_id=2, has_side_effects=True, vmem_limit_bytes=66_000_000,
         ),
-    )(index, ends, x, targets, weight)
+    )(row_places, col_places, index, ends, times, x, targets)
 
 
 def spread_kernel(index_ref, t_ref, image_ref, out_ref):
+    wide = t_ref.shape[1] // BLOCK
+    first = pl.program_id(0) * wide
+    count = image_ref.shape[0]
+
     def one(c, carry):
         place = pl.ds(pl.multiple_of(c * BLOCK, BLOCK), BLOCK)
-        out_ref[:, place] = t_ref[:, place].astype(F32) - image_ref[index_ref[c]]
+        held = index_ref[first + c]
+        keep = jnp.where(held < count, 1.0, 0.0)
+        out_ref[:, place] = t_ref[:, place].astype(F32) - keep * image_ref[jnp.minimum(held, count - 1)].astype(F32)
         return carry
 
-    lax.fori_loop(0, index_ref.shape[0], one, 0, unroll=2)
+    lax.fori_loop(0, wide, one, 0, unroll=2)
 
 
 def spread(index, targets, image):
+    samples, taxa = targets.shape
+    wide = taxa // STEPS
     return pl.pallas_call(
         spread_kernel,
+        grid=(STEPS,),
         out_shape=jax.ShapeDtypeStruct(targets.shape, F32),
-        in_specs=[SCALARS, WHOLE, WHOLE],
-        out_specs=WHOLE,
+        in_specs=[SCALARS, pl.BlockSpec((samples, wide), lambda i: (0, i)), WHOLE],
+        out_specs=pl.BlockSpec((samples, wide), lambda i: (0, i)),
     )(index, targets, image)
 
 
@@ -447,17 +539,8 @@
     count = shard * row_count
     run = count // col_count
     ridge = RIDGE_SHARE * sample_count * row_count
-    weight = jnp.broadcast_to(
-        (0.5 + times.astype(F32) / T_STEPS)[:, None], (sample_count, BLOCK)
-    )
-    places = jnp.pad(
-        jnp.stack([block_rows, block_cols]), ((0, 6), (0, LANES - shard))
-    )
-    everywhere = gather_small(places, 1)
-    rows_all = everywhere[:, :, 0, :shard].transpose(1, 0, 2).reshape(col_count, count)
-    wanted = lax.dynamic_slice_in_dim(rows_all, my_col * run, run, 1) - my_col * column_count
-    cols_mine = lax.dynamic_index_in_dim(everywhere[:, :, 1, :shard], my_col, 1, keepdims=False)
-    cols = cols_mine.reshape(count) - my_col * column_count
+    row_places, col_places = positions(block_rows, block_cols, column_count, 1)
+    cols = col_places[:, :shard].reshape(count)
 
     number = lax.iota(jnp.int32, count)
     slot = jnp.bitwise_xor(lax.div(number, run), my_col) * run + lax.rem(number, run)
@@ -468,9 +551,10 @@
     held = lax.iota(jnp.int32, column_count)[:, None] == cols[None, :]
     end = jnp.max(jnp.where(held, slot[None, :], -1), axis=1)
     end = jnp.where(end < 0, count, end)
-    index = jnp.stack([wanted.reshape(count), cols, before, final])
-
-    image, coeffs = fit(index, (final == slot).astype(F32), samples_x, targets, weight, run, ridge, shard)
+    index = jnp.stack([before, final])
+
+    ends = (final == slot).astype(F32)
+    image, coeffs = fit(row_places, col_places, index, ends, times[None], samples_x, targets, run, ridge, shard)
     return (coeffs, spread(end, targets, image))
 
 

time: 173 us -> 160 us (0.925)
  Pallas kernels: 164 us -> 156 us
  local copies, waits for them, and re-layouts: 4.17 us -> 1.78 us
  other arithmetic: 4.1 us -> 1.87 us
    pallas_call x2, Pallas kernels: 22.1 us -> 17.4 us  [the longest x1 10.9 us: positions(): pl.pallas_call(functools.partial(positions_kernel, taken), out_shape=(jax...]
    pallas_call x1, Pallas kernels: 141 us -> 138 us  [fit(): pl.pallas_call(functools.partial(fit_kernel, run, ridge), out_shape=(jax....]
where the time goes in v2:
time: 160 us
  Pallas kernels  156 us (98%)
  other arithmetic  1.87 us (1%)
  local copies, waits for them, and re-layouts  1.78 us (1%)
    pallas_call x1, Pallas kernels, fit(): pl.pallas_call(functools.partial(fit_kernel, run, ridge), out_shape=(jax....  138 us
    pallas_call x1, Pallas kernels, positions(): pl.pallas_call(functools.partial(positions_kernel, taken), out_shape=(jax...  10.9 us
    pallas_call x1, Pallas kernels, spread(): pl.pallas_call(spread_kernel, grid=(STEPS,), out_shape=jax.ShapeDtypeStru...  6.54 us

profile of v2, /device:TPU:0, one launch (start us, length us, event | category | flops | bytes accessed | tf_op | source)
XLA Modules:
  0.0 160.1 jit_solution(9324718576202474553)
XLA Ops:
  0.6 10.9 %shard_map.68 = (s32[8,128]{1,0:T(8,128)}, s32[4,128]{1,0:T(4,128)}) custom-call(s32[1,18]{1,0:T(1,128)} %bitcast.10, s32[1,18]{1,0:T(1,128)} %bitcast.11), custom_call_target="tpu_custom_call" | custom-call | tf_op jit(solution)/shard_map/pallas_call | solution.py:130
  11.5 0.8 eq.31
  12.3 0.1 select_reduce_fusion
  12.4 0.5 compare_select_fusion.1.index_ref
  12.9 0.2 select_reduce_fusion.1
  13.1 0.5 compare_convert_fusion.ends_ref
  13.6 0.6 pad_add_fusion.index_ref
  14.2 138.3 %shard_map.69 = (bf16[72,128,128]{2,1,0:T(8,128)(2,1)}, f32[18,128,128]{2,1,0:T(8,128)}) custom-call(s32[8,128]{1,0:T(8,128)} %get-tuple-element.6.row_ref, s32[4,128]{1,0:T(4,128)} %get-tuple-element.7.col_ref, s32[2,72]{1,0:T(2,128)} %pad_add_fusion.index_ref, f32[72]{0:T(128)} %compare_convert_fusion.ends_ref, s32[1,128]{1,0:T(1,128)} %bitcast.9, ...), custom_call_target="tpu_custom_call" | custom-call | tf_op jit(solution)/shard_map/pallas_call | solution.py:473
  152.5 0.0 copy-start
  152.5 6.5 %shard_map.70 = f32[128,12288]{1,0:T(8,128)} custom-call(s32[96]{0:T(128)} %compare_select_fusion.1.index_ref, bf16[128,12288]{1,0:T(8,128)(2,1)} %t_ref.1, bf16[72,128,128]{2,1,0:T(8,128)(2,1)} %get-tuple-element.9.image_ref), custom_call_target="tpu_custom_call" | custom-call | tf_op jit(solution)/shard_map/pallas_call | solution.py:522
  159.0 0.0 copy-done
  159.0 1.0 copy.8
  (2 shorter events, 0.0 us)
Async XLA Ops:
  152.5 6.6 %copy-start = (f32[18,128,128]{2,1,0:T(8,128)S(1)}, f32[18,128,128]{2,1,0:T(8,128)}, u32[]{:S(2)}) copy-start(f32[18,128,128]{2,1,0:T(8,128)} %get-tuple-element.14) | copy-start | bytes 3538948

commit v3 on v2

--- a/solution.py
+++ b/solution.py
@@ -11,11 +11,12 @@
 T_STEPS = 64
 RIDGE_SHARE = 0.2
 LANES = 128
-SIZE = 3
-LEAD = 4
-FAR = 6
-LATE = 1
-STEPS = 4
+SIZE = 1
+LEAD = 6
+FAR = 11
+EDGE = 24
+LATE = 2
+PARTS = 6
 VMEM = pltpu.VMEM
 F32 = jnp.float32
 BF16 = jnp.bfloat16
@@ -163,7 +164,7 @@
 
 
 def fit_kernel(
-    run, ridge, row_ref, col_ref, index_ref, ends_ref, times_ref, x_hbm, t_hbm, image_hbm, coeffs_ref,
+    run, ridge, row_ref, col_ref, index_ref, ends_ref, last_ref, times_ref, x_hbm, t_hbm, residual_hbm, coeffs_ref,
     x_ref, t_ref, w_ref, image_ref, give, x_all, near_sum, far_sum, arrived, d_ref, low_ref, s_ref, acc, scal, mine, by_col, line, by_row,
     send_x, recv_x, send_z, recv_z, send_c, recv_c, send_r, recv_r, credit, load, leave,
 ):
@@ -265,24 +266,19 @@
                 far_sum[b] = (far_sum[b].astype(F32) + arrived[far, b].astype(F32)).astype(BF16)
             back(p).start()
 
-    def sweep(make, settle, hooks, last):
+    lag = jnp.where(at_end, EDGE, FAR)
+
+    def sweep(make, settle, hooks, late):
         def body(q, carry):
             pl.when(q < pieces)(lambda: make(q))
             pl.when(has_near & (q >= LEAD) & (q < pieces + LEAD))(lambda: pass_forth(q - LEAD))
-            pl.when((q >= FAR) & (q < pieces + FAR))(lambda: pass_back(q - FAR))
+            pl.when((q >= lag) & (q < pieces + lag))(lambda: pass_back(q - lag))
             for when, hook in hooks:
                 pl.when(q == when)(hook)
-            pl.when(q >= last)(lambda: settle(q - last))
+            pl.when((q >= lag + late) & (q < pieces + lag + late))(lambda: settle(q - lag - late))
             return carry
 
-        lax.fori_loop(0, pieces + last, body, 0)
-
-        def drain(p, carry):
-            forth(p).wait_send()
-            pl.when(has_near)(lambda: back(p).wait_send())
-            return carry
-
-        lax.fori_loop(0, pieces, drain, 0)
+        lax.fori_loop(0, pieces + EDGE + late, body, 0)
 
     def over_col(a, k):
         return push(mine.at[a], by_col.at[a, my_col], send_c.at[a, k - 1], recv_c.at[a, k - 1], "col", k)
@@ -344,6 +340,7 @@
         store_terms(p, terms)
 
     def first_settle(p):
+        forth(p).wait_send()
         base = listed(p)
         made = []
         for j in range(SIZE):
@@ -362,10 +359,7 @@
             s_ref[b] = image
             acc[2] += ends_ref[base + j] * fold(w_ref[...] * image * image)
 
-    sweep(first_make, first_settle, later, FAR)
-    for s in range(1, cols):
-        exchange(s).wait_send()
-
+    sweep(first_make, first_settle, later, 0)
     def greet(other):
         pl.semaphore_signal(credit, inc=1, device_id={"row": other}, device_id_type=MESH)
 
@@ -388,6 +382,7 @@
         scal[4:5] = wide(square)
 
     def second_make(p):
+        pl.when(has_near)(lambda: back(p).wait_send())
         base = listed(p)
         terms = []
         for j in range(SIZE):
@@ -396,6 +391,7 @@
         store_terms(p, terms)
 
     def second_settle(p):
+        forth(p).wait_send()
         base = listed(p)
         alpha, shift = scal[0:1], scal[1:2]
         made = []
@@ -420,11 +416,21 @@
             acc[6] += final * fold(weighted * image)
             acc[7] += final * fold(weighted * s_ref[b])
 
-    last = FAR + LATE
     sweep(second_make, second_settle,
-          [(LEAD - 1, lambda: reduce_middle(0)), (last, first_scalars)], last)
+          [(LEAD - 1, lambda: reduce_middle(0)), (FAR + LATE, first_scalars)], LATE)
 
     reduce_start(1, (3, 4, 5, 6, 7))
+    for s in range(1, cols):
+        exchange(s).wait_send()
+
+    @pl.when(has_near)
+    def _():
+        def drain(p, carry):
+            back(p).wait_send()
+            return carry
+
+        lax.fori_loop(0, pieces, drain, 0)
+
     reduce_middle(1)
     total = reduce_end(1)
     alpha, gamma = scal[0:1], scal[2:3]
@@ -436,18 +442,22 @@
     alpha_next = gamma_next / (square_next + ridge * flat_next)
     mixed = alpha + alpha_next * beta
 
-    def leaving(s):
-        place = pl.ds(s * run, run)
-        return pltpu.make_async_copy(give.at[place], image_hbm.at[place], leave.at[s])
-
-    for s in range(cols):
-        def mix(i, carry):
-            b = s * run + i
-            give[b] = (mixed * s_ref[b] + alpha_next * image_ref[b]).astype(BF16)
+    wide_part = t_ref.shape[1] // PARTS
+
+    def leaving(k):
+        place = pl.ds(k * wide_part, wide_part)
+        return pltpu.make_async_copy(t_ref.at[:, place], residual_hbm.at[:, place], leave.at[k])
+
+    for k in range(PARTS):
+        def column(i, carry):
+            c = k * (wide_part // BLOCK) + i
+            place = pl.ds(pl.multiple_of(c * BLOCK, BLOCK), BLOCK)
+            fitted = mixed * s_ref[last_ref[c]] + alpha_next * image_ref[last_ref[c]]
+            t_ref[:, place] = (t_ref[:, place].astype(F32) - fitted).astype(BF16)
             return carry
 
-        lax.fori_loop(0, run, mix, 0, unroll=3)
-        leaving(s).start()
+        lax.fori_loop(0, wide_part // BLOCK, column, 0, unroll=2)
+        leaving(k).start()
 
     runs = coeffs_ref.shape[0] // run
     for u in range(runs):
@@ -459,11 +469,11 @@
             return carry
 
         lax.fori_loop(0, run, own, 0)
-    for s in range(cols):
-        leaving(s).wait()
-
-
-def fit(row_places, col_places, index, ends, times, x, targets, run, ridge, shard):
+    for k in range(PARTS):
+        leaving(k).wait()
+
+
+def fit(row_places, col_places, index, ends, last, times, x, targets, run, ridge, shard):
     cols, rows = lax.axis_size("col"), lax.axis_size("row")
     count = run * cols
     samples = x.shape[0]
@@ -473,10 +483,10 @@
     return pl.pallas_call(
         functools.partial(fit_kernel, run, ridge),
         out_shape=(
-            jax.ShapeDtypeStruct((count, samples, BLOCK), BF16),
+            jax.ShapeDtypeStruct(x.shape, BF16),
             jax.ShapeDtypeStruct((shard,) + block, F32),
         ),
-        in_specs=[SCALARS, SCALARS, SCALARS, SCALARS, WHOLE, APART, APART],
+        in_specs=[SCALARS] * 5 + [WHOLE, APART, APART],
         out_specs=(APART, WHOLE),
         scratch_shapes=[
             VMEM(x.shape, BF16), VMEM(x.shape, BF16), VMEM((samples, BLOCK), F32),
@@ -493,39 +503,12 @@
             dma((2, pieces)), dma((2, pieces)),
             dma((2, cols - 1)), dma((2, cols - 1)),
             dma((2, rows - 1)), dma((2, rows - 1)),
-            pltpu.SemaphoreType.REGULAR, dma((2,)), dma((cols,)),
+            pltpu.SemaphoreType.REGULAR, dma((2,)), dma((PARTS,)),
         ],
         compiler_params=pltpu.CompilerParams(
             collective_id=2, has_side_effects=True, vmem_limit_bytes=66_000_000,
         ),
-    )(row_places, col_places, index, ends, times, x, targets)
-
-
-def spread_kernel(index_ref, t_ref, image_ref, out_ref):
-    wide = t_ref.shape[1] // BLOCK
-    first = pl.program_id(0) * wide
-    count = image_ref.shape[0]
-
-    def one(c, carry):
-        place = pl.ds(pl.multiple_of(c * BLOCK, BLOCK), BLOCK)
-        held = index_ref[first + c]
-        keep = jnp.where(held < count, 1.0, 0.0)
-        out_ref[:, place] = t_ref[:, place].astype(F32) - keep * image_ref[jnp.minimum(held, count - 1)].astype(F32)
-        return carry
-
-    lax.fori_loop(0, wide, one, 0, unroll=2)
-
-
-def spread(index, targets, image):
-    samples, taxa = targets.shape
-    wide = taxa // STEPS
-    return pl.pallas_call(
-        spread_kernel,
-        grid=(STEPS,),
-        out_shape=jax.ShapeDtypeStruct(targets.shape, F32),
-        in_specs=[SCALARS, pl.BlockSpec((samples, wide), lambda i: (0, i)), WHOLE],
-        out_specs=pl.BlockSpec((samples, wide), lambda i: (0, i)),
-    )(index, targets, image)
+    )(row_places, col_places, index, ends, last, times, x, targets)
 
 
 def on_device(samples_x, targets, times, block_rows, block_cols):
@@ -554,8 +537,8 @@
     index = jnp.stack([before, final])
 
     ends = (final == slot).astype(F32)
-    image, coeffs = fit(row_places, col_places, index, ends, times[None], samples_x, targets, run, ridge, shard)
-    return (coeffs, spread(end, targets, image))
+    residual, coeffs = fit(row_places, col_places, index, ends, end, times[None], samples_x, targets, run, ridge, shard)
+    return (coeffs, residual.astype(F32))
 
 
 def solution(mesh):

time: 160 us -> 157 us (0.981)
  Pallas kernels: 156 us -> 147 us
  other arithmetic: 1.87 us -> 7.23 us
    pallas_call x1 -> x0, Pallas kernels: 6.54 us -> none  [spread(): pl.pallas_call(spread_kernel, grid=(STEPS,), out_shape=jax.ShapeDtypeStru...]
    convert_element_type x0 -> x1, other arithmetic: none -> 5.33 us  [on_device(): return (coeffs, residual.astype(F32))]
    pallas_call x1, Pallas kernels: 138 us -> 136 us  [fit(): pl.pallas_call(functools.partial(fit_kernel, run, ridge), out_shape=(jax....]
where the time goes in v3:
time: 157 us
  Pallas kernels  147 us (94%)
  other arithmetic  7.23 us (5%)
  local copies, waits for them, and re-layouts  1.76 us (1%)
    pallas_call x1, Pallas kernels, fit(): pl.pallas_call(functools.partial(fit_kernel, run, ridge), out_shape=(jax....  136 us
    pallas_call x1, Pallas kernels, positions(): pl.pallas_call(functools.partial(positions_kernel, taken), out_shape=(jax...  10.9 us
    convert_element_type x1, other arithmetic, on_device(): return (coeffs, residual.astype(F32))  5.33 us

profile of v3, /device:TPU:0, one launch (start us, length us, event | category | flops | bytes accessed | tf_op | source)
XLA Modules:
  0.0 156.9 jit_solution(4768995407136003864)
XLA Ops:
  0.6 10.9 %shard_map.68 = (s32[8,128]{1,0:T(8,128)}, s32[4,128]{1,0:T(4,128)}) custom-call(s32[1,18]{1,0:T(1,128)} %bitcast.10, s32[1,18]{1,0:T(1,128)} %bitcast.11), custom_call_target="tpu_custom_call" | custom-call | tf_op jit(solution)/shard_map/pallas_call | solution.py:131
  11.5 0.7 eq.31
  12.3 0.1 select_reduce_fusion
  12.4 0.5 compare_select_fusion.1.last_ref
  12.9 0.2 select_reduce_fusion.1
  13.1 0.5 compare_convert_fusion.ends_ref
  13.6 0.6 pad_add_fusion.index_ref
  14.2 136.4 %shard_map.69 = (bf16[128,12288]{1,0:T(8,128)(2,1)}, f32[18,128,128]{2,1,0:T(8,128)}) custom-call(s32[8,128]{1,0:T(8,128)} %get-tuple-element.6.row_ref, s32[4,128]{1,0:T(4,128)} %get-tuple-element.7.col_ref, s32[2,72]{1,0:T(2,128)} %pad_add_fusion.index_ref, f32[72]{0:T(128)} %compare_convert_fusion.ends_ref, s32[96]{0:T(128)} %compare_select_fusion.1.last_ref, ...), custom_call_target="tpu_custom_call" | custom-call | tf_op jit(solution)/shard_map/pallas_call | solution.py:483
  150.6 0.0 copy-start
  150.6 5.3 %convert_element_type.7 = f32[128,12288]{1,0:T(8,128)} convert(bf16[128,12288]{1,0:T(8,128)(2,1)} %get-tuple-element.9) | non-fusion elementwise | flops 1572864 | bytes 9437184 | tf_op jit(solution)/shard_map/convert_element_type | solution.py:541
  155.9 0.0 copy-done
  155.9 1.0 copy.8
  (2 shorter events, 0.0 us)
Async XLA Ops:
  150.6 5.3 %copy-start = (f32[18,128,128]{2,1,0:T(8,128)S(1)}, f32[18,128,128]{2,1,0:T(8,128)}, u32[]{:S(2)}) copy-start(f32[18,128,128]{2,1,0:T(8,128)} %get-tuple-element.14) | copy-start | bytes 3538948
